TPU v7x, 32 devices: a whole 2x2x4 slice. The times are simulated.
32 devices in a mesh: dp: 4 (over y, core), cells: 8 (over z, x).
Axes of the slice: x: 2, y: 2, z: 4, core: 2. Of those that a mesh axis runs over, the one named last changes fastest.
Arguments:
- sensitivity: float32 [8192, 12288], P('dp', 'cells'), may hold values from -0.0546875 to 0.0546875
- observed: float32 [8192, 256], P('dp'), may hold values from -6 to 6
- models: float32 [12288, 256], P('cells'), may hold values from -6 to 6
- neighbour_map: int32 [4, 768], replicated, may hold values from 0 to 767, as said below
- edge_mask: int32 [12288], P('cells'), may hold values 0 or 1
Outputs:
- updated: float32 [12288, 256], P('cells')
Inputs may be any that keep to these rules, and one draw needn't show every extreme that they name: `neighbour_map`: each row k maps every cell of a periodic 32 by 24 plane grid, numbered in a drawn order, to its neighbour in one of the four grid directions; every row is a permutation.
All inputs are finite; a program needn't handle non-finite values. No bound on the sum of `edge_mask` on one device may be relied on, other than what follows from the above.
Results may differ from a plain program's by a relative error of at most 0.0001.
Values sent between devices are 32-bit elements; how exact they have to be, the bound alone decides.
A program may use at most 128 MiB of HBM per device.

v0:
```python
import jax
import jax.numpy as jnp
from jax import lax
from jax.sharding import PartitionSpec as P

ITERS = 2


def with_halo(cells, sides, width):
    for axis, dim in sides:
        count = lax.axis_size(axis)
        ends = count - 1
        head = lax.slice_in_dim(cells, 0, width, axis=dim)
        tail = lax.slice_in_dim(cells, cells.shape[dim] - width, cells.shape[dim], axis=dim)
        cells = jnp.concatenate(
            [
                lax.ppermute(tail, axis, [(i, (i + 1) % count) for i in range(ends)]),
                cells,
                lax.ppermute(head, axis, [((i + 1) % count, i) for i in range(ends)]),
            ],
            axis=dim,
        )
    return cells


def reweight(misfit):
    return misfit / jnp.maximum(jnp.abs(misfit), 1.0)


def smooth_local(current, neighbour_map, edge_mask):
    plane_cells = neighbour_map.shape[1]
    count = current.shape[0] // plane_cells
    planes = current.reshape(count, plane_cells, current.shape[1])
    padded = with_halo(planes, (("cells", 0),), 1)
    total = jnp.zeros_like(planes)
    for other in (padded[:-2], padded[2:]):
        diff = other - planes
        total = total + diff / jnp.sqrt(1.0 + diff * diff)
    for k in range(4):
        other = jnp.take(planes, neighbour_map[k], axis=1)
        diff = other - planes
        total = total + diff / jnp.sqrt(1.0 + diff * diff)
    scale = 1.0 - 0.75 * edge_mask.astype(jnp.float32).reshape(count, plane_cells, 1)
    return (total * scale).reshape(current.shape)


def local(sensitivity, observed, models, neighbour_map, edge_mask):
    current = models
    for step in range(ITERS):
        predicted = lax.psum(
            jnp.dot(
                sensitivity,
                current,
                precision=lax.Precision.HIGHEST,
                preferred_element_type=jnp.float32,
            ),
            "cells",
        )
        weighted = reweight(predicted - observed)
        smooth = smooth_local(current, neighbour_map, edge_mask)
        partial_grad = lax.dot_general(
            sensitivity,
            weighted,
            (((0,), (0,)), ((), ())),
            precision=lax.Precision.HIGHEST,
            preferred_element_type=jnp.float32,
        )
        gradient = lax.psum(partial_grad, "dp")
        current = current - 1.0 * gradient + 0.05 * smooth
    return current


def solution(mesh):
    return jax.shard_map(
        local,
        mesh=mesh,
        in_specs=(P("dp", "cells"), P("dp", None), P("cells", None), P(), P("cells")),
        out_specs=P("cells", None),
        check_vma=False,
    )
```

profile of v0, /device:TPU:0, one launch (start us, length us, event | category | flops | bytes accessed | tf_op | source)
XLA Modules:
  0.0 418.7 jit_solution(4675436302633939359)
XLA Ops:
  6.5 13.9 %fusion.16 = f32[2048,256]{1,0:T(8,128)} fusion(f32[2048,1536]{1,0:T(8,128)} %param.7, f32[1536,256]{1,0:T(8,128)} %param.9), kind=kOutput, calls=%fused_computation.72 | convolution fusion | flops 9663676416 | bytes 16252928 | tf_op jit(solution)/shard_map/dot_general | solution.py:51
  20.6 1.3 copy-done
  23.1 5.7 %collective-permute-start = (f32[1,768,256]{2,1,0:T(8,128)}, f32[1,768,256]{2,1,0:T(8,128)}, u32[]{:S(2)}, u32[]{:S(2)}) collective-permute-start(f32[1,768,256]{2,1,0:T(8,128)} %get-tuple-element.12), channel_id=1, source_target_pairs={{0,1},{1,2},{2,3},{3,4},{4,5},{5,6},{6,7},{8,9},{9,10},{10,11},{11... | collective-permute-start | bytes 2359304 | tf_op jit(solution)/shard_map/ppermute | solution.py:17
  31.5 4.0 gather_fusion.3
  35.5 4.0 gather_fusion.2
  39.6 4.0 gather_fusion.1
  43.6 4.1 gather_fusion
  47.7 96.1 %all-reduce.5.cloned.1.call-done = f32[2048,256]{1,0:T(8,128)} async-done(((f32[2048,256]{1,0:T(8,128)}), f32[2048,256]{1,0:T(8,128)}) %all-reduce.5.cloned.1.call-update) | async-done | bytes 2097168 | tf_op jit(solution)/shard_map/psum | solution.py:50
  143.8 24.7 %convolution_bitcast_fusion.2 = f32[1536,256]{1,0:T(8,128)} fusion(f32[2048,1536]{1,0:T(8,128)} %param.7, f32[2048,256]{1,0:T(8,128)} %all-reduce.5.cloned.1.call-done, f32[2048,256]{1,0:T(8,128)} %param.8), kind=kOutput, calls=%fused_computation.10 | convolution fusion | flops 9665773568 | bytes 18350080 | tf_op jit(solution)/shard_map/dot_general | solution.py:61
  169.9 6.3 %multiply_multiply_fusion.1 = f32[2,768,256]{2,1,0:T(8,128)} fusion(f32[2,768,256]{2,1,0:T(8,128)S(1)} %bitcast.61, f32[768,2,256]{2,1,0:T(2,128)S(1)} %copy-done.1, f32[768,2,256]{2,1,0:T(2,128)} %gather_fusion.2, f32[768,2,256]{2,1,0:T(2,128)} %gather_fusion.1, f32[768,2,256]{2,1,0:T(2,128)} %gather_fusion, f32[1,768,256]{2,1,0:T(8,128)} %collective-permute-done.1, ...), kind=kLoop, calls=%fused_computation.46 | loop fusion | flops 14548992 | bytes 11019264 | tf_op jit(solution)/shard_map/mul | solution.py:69
  176.2 34.6 %all-reduce.7.cloned.1.call-done = f32[1536,256]{1,0:T(8,128)} async-done(((f32[1536,256]{1,0:T(8,128)}), f32[1536,256]{1,0:T(8,128)}) %all-reduce.7.cloned.1.call-update) | async-done | bytes 1572880 | tf_op jit(solution)/shard_map/psum | solution.py:68
  210.8 2.2 bitcast_add_fusion.1
  213.0 13.5 %convolution_bitcast_fusion.1 = f32[2048,256]{1,0:T(8,128)} fusion(f32[1536,256]{1,0:T(8,128)S(1)} %bitcast_add_fusion.1, f32[2048,1536]{1,0:T(8,128)} %param.7), kind=kOutput, calls=%fused_computation.9 | convolution fusion | flops 9663676416 | bytes 16252928 | tf_op jit(solution)/shard_map/dot_general | solution.py:51
  227.8 4.0 gather_fusion.7
  231.8 4.0 gather_fusion.6
  235.8 4.0 gather_fusion.5
  239.9 4.1 gather_fusion.4
  245.2 4.2 %collective-permute-start.2 = (f32[1,768,256]{2,1,0:T(8,128)}, f32[1,768,256]{2,1,0:T(8,128)}, u32[]{:S(2)}, u32[]{:S(2)}) collective-permute-start(f32[1,768,256]{2,1,0:T(8,128)} %get-tuple-element.10), channel_id=1, source_target_pairs={{0,1},{1,2},{2,3},{3,4},{4,5},{5,6},{6,7},{8,9},{9,10},{10,11},{11... | collective-permute-start | bytes 2359304 | tf_op jit(solution)/shard_map/ppermute | solution.py:17
  250.7 90.6 %all-reduce.9.cloned.1.call-done = f32[2048,256]{1,0:T(8,128)} async-done(((f32[2048,256]{1,0:T(8,128)}), f32[2048,256]{1,0:T(8,128)}) %all-reduce.9.cloned.1.call-update) | async-done | bytes 2097168 | tf_op jit(solution)/shard_map/psum | solution.py:50
  341.3 24.8 %convolution_bitcast_fusion = f32[1536,256]{1,0:T(8,128)} fusion(f32[2048,1536]{1,0:T(8,128)} %param.7, f32[2048,256]{1,0:T(8,128)} %all-reduce.9.cloned.1.call-done, f32[2048,256]{1,0:T(8,128)} %param.8), kind=kOutput, calls=%fused_computation.8 | convolution fusion | flops 9665773568 | bytes 18350080 | tf_op jit(solution)/shard_map/dot_general | solution.py:61
  366.1 1.4 copy-done.2
  367.5 6.1 %multiply_multiply_fusion = f32[2,768,256]{2,1,0:T(8,128)} fusion(f32[2,768,256]{2,1,0:T(8,128)S(1)} %bitcast.59, f32[768,2,256]{2,1,0:T(2,128)S(1)} %copy-done.2, f32[768,2,256]{2,1,0:T(2,128)} %gather_fusion.6, f32[768,2,256]{2,1,0:T(2,128)} %gather_fusion.5, f32[768,2,256]{2,1,0:T(2,128)} %gather_fusion.4, f32[1,768,256]{2,1,0:T(8,128)} %collective-permute-done.3, ...), kind=kLoop, calls=%fused_computation.45 | loop fusion | flops 14548992 | bytes 11019264 | tf_op jit(solution)/shard_map/mul | solution.py:69
  373.6 34.8 %all-reduce.11.cloned.1.call-done = f32[1536,256]{1,0:T(8,128)} async-done(((f32[1536,256]{1,0:T(8,128)}), f32[1536,256]{1,0:T(8,128)}) %all-reduce.11.cloned.1.call-update) | async-done | bytes 1572880 | tf_op jit(solution)/shard_map/psum | solution.py:68
  408.4 3.3 bitcast_add_fusion
  (37 shorter events, 9.2 us)
Async XLA Ops:
  6.5 137.2 %all-reduce.5.cloned.1.call-start = ((), (), s32[]{:S(2)}) async-start(), calls=%async_computation | async-start | bytes 4194304 | tf_op jit(solution)/shard_map/psum | solution.py:50
  20.5 1.4 copy-start
  20.5 9.7 %copy-start.4 = (s32[1536]{0:T(1024)S(1)}, s32[1536]{0:T(1024)}, u32[]{:S(2)}) copy-start(s32[1536]{0:T(1024)} %param.11) | copy-start | bytes 18436
  20.5 190.3 %all-reduce.7.cloned.1.call-start = ((), (), s32[]{:S(2)}) async-start(), calls=%async_computation.1 | async-start | bytes 3145728 | tf_op jit(solution)/shard_map/psum | solution.py:68
  23.1 145.4 %collective-permute-start = (f32[1,768,256]{2,1,0:T(8,128)}, f32[1,768,256]{2,1,0:T(8,128)}, u32[]{:S(2)}, u32[]{:S(2)}) collective-permute-start(f32[1,768,256]{2,1,0:T(8,128)} %get-tuple-element.12), channel_id=1, source_target_pairs={{0,1},{1,2},{2,3},{3,4},{4,5},{5,6},{6,7},{8,9},{9,10},{10,11},{11... | collective-permute-start | bytes 2359304 | tf_op jit(solution)/shard_map/ppermute | solution.py:17
  28.9 139.7 %collective-permute-start.1 = (f32[1,768,256]{2,1,0:T(8,128)}, f32[1,768,256]{2,1,0:T(8,128)}, u32[]{:S(2)}, u32[]{:S(2)}) collective-permute-start(f32[1,768,256]{2,1,0:T(8,128)} %get-tuple-element.13), channel_id=1, source_target_pairs={{1,0},{2,1},{3,2},{4,3},{5,4},{6,5},{7,6},{9,8},{10,9},{11,10},{12... | collective-permute-start | bytes 2359304 | tf_op jit(solution)/shard_map/ppermute | solution.py:19
  30.2 1.2 copy-start.3
  168.5 1.4 copy-start.1
  168.5 172.8 %all-reduce.9.cloned.1.call-start = ((), (), s32[]{:S(2)}) async-start(), calls=%async_computation.2 | async-start | bytes 4194304 | tf_op jit(solution)/shard_map/psum | solution.py:50
  226.5 181.9 %all-reduce.11.cloned.1.call-start = ((), (), s32[]{:S(2)}) async-start(), calls=%async_computation.3 | async-start | bytes 3145728 | tf_op jit(solution)/shard_map/psum | solution.py:68
  245.2 120.9 %collective-permute-start.2 = (f32[1,768,256]{2,1,0:T(8,128)}, f32[1,768,256]{2,1,0:T(8,128)}, u32[]{:S(2)}, u32[]{:S(2)}) collective-permute-start(f32[1,768,256]{2,1,0:T(8,128)} %get-tuple-element.10), channel_id=1, source_target_pairs={{0,1},{1,2},{2,3},{3,4},{4,5},{5,6},{6,7},{8,9},{9,10},{10,11},{11... | collective-permute-start | bytes 2359304 | tf_op jit(solution)/shard_map/ppermute | solution.py:17
  249.4 116.7 %collective-permute-start.3 = (f32[1,768,256]{2,1,0:T(8,128)}, f32[1,768,256]{2,1,0:T(8,128)}, u32[]{:S(2)}, u32[]{:S(2)}) collective-permute-start(f32[1,768,256]{2,1,0:T(8,128)} %get-tuple-element.11), channel_id=1, source_target_pairs={{1,0},{2,1},{3,2},{4,3},{5,4},{6,5},{7,6},{9,8},{10,9},{11,10},{12... | collective-permute-start | bytes 2359304 | tf_op jit(solution)/shard_map/ppermute | solution.py:19
  366.1 1.4 copy-start.2
Sparse Core Ops, SparseCore 0:
  20.6 123.0 all-reduce.4
  168.6 42.1 all-reduce.6
  226.7 114.5 all-reduce.8
  366.2 42.1 all-reduce.10
where the time goes:
time: 426 us; the launch traced here: 419 us
  waiting for transfers between devices  256 us (60%)
  matrix products  77 us (18%)
  local copies, waits for them, and re-layouts  41.2 us (10%)
  other arithmetic  17.9 us (4%)
  between operations  13.7 us (3%)
  starting transfers between devices  12.6 us (3%)
    psum x2, waiting for transfers between devices, local(): lax.psum(jnp.dot(sensitivity, current, precision=lax.Precision.HIGHEST, p...  187 us
    psum x2, waiting for transfers between devices, local(): gradient = lax.psum(partial_grad, 'dp')  69.5 us
    dot_general x2, matrix products, local(): lax.dot_general(sensitivity, weighted, (((0,), (0,)), ((), ())), precisio...  49.5 us
    gather x8, local copies, waits for them, and re-layouts, smooth_local(): other = jnp.take(planes, neighbour_map[k], axis=1)  32.2 us
    dot_general x2, matrix products, local(): jnp.dot(sensitivity, current, precision=lax.Precision.HIGHEST, preferred_...  27.5 us
    mul x2, other arithmetic, local(): current = current - 1.0 * gradient + 0.05 * smooth  12.4 us
    ppermute x2, starting transfers between devices, with_halo(): lax.ppermute(tail, axis, [(i, (i + 1) % count) for i in range(ends)])  9.95 us
  transfers between devices with their start and end apart: 8, of which 4 were waited for; matrix products, arithmetic and copies ran while one was open for 24% of the time, Pallas kernels for 0%

commit v1 on v0

v1 whole, which is shorter than its diff:
```python
import functools

import jax
import jax.numpy as jnp
from jax import lax
from jax.experimental import pallas as pl
from jax.experimental.pallas import tpu as pltpu
from jax.sharding import PartitionSpec as P

ITERS = 2
CHUNK = 128
PARTS = 2
F32 = jnp.float32
BF16 = jnp.bfloat16


def split(x):
    hi = x.astype(BF16)
    return hi, (x - hi.astype(F32)).astype(BF16)


def bits_of(count):
    return count.bit_length() - 1


def dot(a, b, dims):
    return lax.dot_general(a, b, (dims, ((), ())), preferred_element_type=F32)


def aligned(start, size):
    return pl.ds(pl.multiple_of(start, 8), size)


class Halving:
    def __init__(self, axis, count, rows, sends, recvs):
        self.axis, self.rows = axis, rows
        self.bits = bits_of(count)
        self.sends, self.recvs = sends, recvs
        me = lax.axis_index(axis)
        self.bit = [(me // 2**b) % 2 for b in range(self.bits)]
        self.partner = [me + (1 - 2 * self.bit[b]) * 2**b for b in range(self.bits)]
        self.off, self.size = [0], [rows]
        for b in range(self.bits):
            half = self.size[b] // 2
            self.off.append(self.off[b] + self.bit[b] * half)
            self.size.append(half)

    def reduce(self, data, land, chunk, b):
        half = self.size[b + 1]
        away = self.off[b] + (1 - self.bit[b]) * half
        return pltpu.make_async_remote_copy(
            src_ref=data.at[aligned(chunk * self.rows + away, half)],
            dst_ref=land.at[aligned(chunk * self.rows + self.rows - self.size[b], half)],
            send_sem=self.sends.at[b, chunk],
            recv_sem=self.recvs.at[b, chunk],
            device_id={self.axis: self.partner[b]},
            device_id_type=pl.DeviceIdType.MESH,
        )

    def kept(self, chunk, b):
        return aligned(chunk * self.rows + self.off[b + 1], self.size[b + 1])

    def landed(self, chunk, b):
        return aligned(chunk * self.rows + self.rows - self.size[b], self.size[b + 1])

    def gather(self, data, chunk, b):
        here = data.at[self.kept(chunk, b)]
        return pltpu.make_async_remote_copy(
            src_ref=here,
            dst_ref=here,
            send_sem=self.sends.at[self.bits + b, chunk],
            recv_sem=self.recvs.at[self.bits + b, chunk],
            device_id={self.axis: self.partner[b]},
            device_id_type=pl.DeviceIdType.MESH,
        )

    def stage(self, s, chunk, data, land, result, finish):
        bits = self.bits
        if s > 0 and s <= bits:
            self.reduce(data, land, chunk, s - 1).wait()
            kept = self.kept(chunk, s - 1)
            total = data[kept, :] + land[self.landed(chunk, s - 1), :]
            if s < bits:
                data[kept, :] = total
            else:
                finish(chunk, kept, total)
        elif s > bits:
            self.gather(result, chunk, 2 * bits - s).wait()
        if s < bits:
            self.reduce(data, land, chunk, s).start()
        elif s < 2 * bits:
            self.gather(result, chunk, 2 * bits - 1 - s).start()


def body(sizes, plane, sens_hbm, obs_ref, models_ref, near_ref, mask_ref, out_ref,
         sens, part, land, weighted, grad, gland, middle, high, low, smooth,
         under, over, load_sem, c_send, c_recv, d_send, d_recv, h_send, h_recv):
    n_dp, n_cells = sizes
    ndata, ncell = sens.shape
    me = lax.axis_index("cells")
    rows = part.shape[0] // c_send.shape[1]
    chunks = ndata // rows
    parts = d_send.shape[1]
    prow = ncell // parts
    per_plane = plane // prow
    cells = Halving("cells", n_cells, rows, c_send, c_recv)
    dp = Halving("dp", n_dp, prow, d_send, d_recv)
    seg = dp.size[-1]
    own = dp.off[-1]

    def load(c):
        at = aligned(c * rows, rows)
        return pltpu.make_async_copy(sens_hbm.at[at], sens.at[at], load_sem.at[c])

    for c in range(chunks):
        load(c).start()

    barrier = pltpu.get_barrier_semaphore()

    def greet(where):
        pl.semaphore_signal(barrier, inc=1, device_id=where, device_id_type=pl.DeviceIdType.MESH)

    for b in range(cells.bits):
        greet({"cells": cells.partner[b]})
    for b in range(dp.bits):
        greet({"dp": dp.partner[b]})

    has_under, has_over = me > 0, me < n_cells - 1

    @pl.when(has_under)
    def _():
        greet({"cells": me - 1})

    @pl.when(has_over)
    def _():
        greet({"cells": me + 1})

    @pl.when(me == 0)
    def _():
        under[...] = jnp.zeros_like(under)

    @pl.when(me == n_cells - 1)
    def _():
        over[...] = jnp.zeros_like(over)

    pl.semaphore_wait(
        barrier,
        cells.bits + dp.bits + (me + n_cells - 1) // n_cells + (2 * n_cells - 2 - me) // n_cells,
    )

    states = [models_ref] + [middle] * (ITERS - 1) + [out_ref]

    def halo(current, step, i, upward):
        source = (ncell - plane if upward else 0) + i * prow + own
        return pltpu.make_async_remote_copy(
            src_ref=current.at[aligned(source, seg)],
            dst_ref=(under if upward else over).at[step, pl.ds(i * seg, seg)],
            send_sem=h_send.at[step, int(upward), i],
            recv_sem=h_recv.at[step, int(upward), i],
            device_id={"cells": me + 1 if upward else me - 1},
            device_id_type=pl.DeviceIdType.MESH,
        )

    def halos(current, step, act_over, act_under):
        @pl.when(has_over)
        def _():
            for i in range(per_plane):
                act_over(i)

        @pl.when(has_under)
        def _():
            for i in range(per_plane):
                act_under(i)

    for step in range(ITERS):
        current, later = states[step], states[step + 1]

        halos(
            current, step,
            lambda i: halo(current, step, i, True).start(),
            lambda i: halo(current, step, i, False).start(),
        )
        hi, lo = split(current[...])
        high[...] = hi
        low[...] = lo
        grad[...] = jnp.zeros_like(grad)

        def predict(c):
            at = aligned(c * rows, rows)
            if step == 0:
                load(c).wait()
            s_hi, s_lo = split(sens[at, :])
            nn = ((1,), (0,))
            part[at, :] = dot(s_hi, high[...], nn) + dot(s_hi, low[...], nn) + dot(s_lo, high[...], nn)

        def reweight(c, kept, total):
            misfit = total - obs_ref[kept, :]
            weighted[kept, :] = misfit / jnp.maximum(jnp.abs(misfit), 1.0)

        def back(c):
            at = aligned(c * rows, rows)
            s_hi, s_lo = split(sens[at, :])
            w_hi, w_lo = split(weighted[at, :])
            tn = ((0,), (0,))
            grad[...] += dot(s_hi, w_hi, tn) + dot(s_hi, w_lo, tn) + dot(s_lo, w_hi, tn)

        def smooth_part(q):
            base = q * prow + own
            inner = lax.rem(base, plane)
            first = base - inner
            cell = current[aligned(base, seg), :]
            total = jnp.zeros_like(cell)

            def add(other):
                diff = other - cell
                return diff / jnp.sqrt(1.0 + diff * diff)

            at = aligned(lax.rem(q, per_plane) * seg, seg)
            below = current[aligned(jnp.maximum(base - plane, 0), seg), :]
            above = current[aligned(jnp.minimum(base + plane, ncell - seg), seg), :]
            total += add(jnp.where(first == 0, under[step, at, :], below))
            total += add(jnp.where(first == ncell - plane, over[step, at, :], above))
            whole = pl.ds(pl.multiple_of(first, 16), plane)
            nn = ((1,), (0,))
            for k in range(4):
                column = near_ref[aligned(inner, seg), k:k + 1]
                pick = column == lax.broadcasted_iota(jnp.int32, (seg, plane), 1)
                pick = jnp.where(pick, 1.0, 0.0).astype(BF16)
                total += add(dot(pick, high[whole, :], nn) + dot(pick, low[whole, :], nn))
            scale = 1.0 - 0.75 * mask_ref[aligned(base, seg), :].astype(F32)
            smooth[aligned(q * seg, seg), :] = total * scale

        predict(0)
        stages = 2 * cells.bits

        def slot(t, carry):
            for s in reversed(range(stages + 1)):
                c = t - s

                @pl.when(jnp.logical_and(c >= 0, c < chunks))
                def _():
                    cells.stage(s, c, part, land, weighted, reweight)

            @pl.when(t + 1 < chunks)
            def _():
                predict(t + 1)

            q = t - 3

            @pl.when(q == 0)
            def _():
                halos(
                    current, step,
                    lambda i: halo(current, step, i, True).wait_send(),
                    lambda i: halo(current, step, i, False).wait_send(),
                )
                halos(
                    current, step,
                    lambda i: halo(current, step, i, False).wait_recv(),
                    lambda i: halo(current, step, i, True).wait_recv(),
                )

            @pl.when(jnp.logical_and(q >= 0, q < parts))
            def _():
                smooth_part(q)

            @pl.when(t >= stages)
            def _():
                back(t - stages)

            return carry

        lax.fori_loop(0, chunks + stages, slot, 0)

        def update(q, kept, total):
            later[kept, :] = current[kept, :] - 1.0 * total + 0.05 * smooth[aligned(q * seg, seg), :]

        def dp_slot(t, carry):
            for s in reversed(range(2 * dp.bits + 1)):
                q = t - s

                @pl.when(jnp.logical_and(q >= 0, q < parts))
                def _():
                    dp.stage(s, q, grad, gland, later, update)

            return carry

        lax.fori_loop(0, parts + 2 * dp.bits, dp_slot, 0)


def invert(n_dp, n_cells, sensitivity, observed, models, neighbour_map, edge_mask):
    ndata, ncell = sensitivity.shape
    sols = models.shape[1]
    plane = neighbour_map.shape[1]
    rows = max(CHUNK, 8 * n_cells)
    chunks = ndata // rows
    parts = ncell // plane * PARTS
    seg = ncell // parts // n_dp
    vmem = pl.BlockSpec(memory_space=pltpu.VMEM)
    dma = pltpu.SemaphoreType.DMA
    nb, nd = 2 * bits_of(n_cells), 2 * bits_of(n_dp)
    return pl.pallas_call(
        functools.partial(body, (n_dp, n_cells), plane),
        out_shape=jax.ShapeDtypeStruct((ncell, sols), F32),
        in_specs=[pl.BlockSpec(memory_space=pl.ANY)] + [vmem] * 4,
        out_specs=vmem,
        scratch_shapes=[
            pltpu.VMEM((ndata, ncell), F32),
            pltpu.VMEM((ndata, sols), F32),
            pltpu.VMEM((ndata, sols), F32),
            pltpu.VMEM((ndata, sols), F32),
            pltpu.VMEM((ncell, sols), F32),
            pltpu.VMEM((ncell, sols), F32),
            pltpu.VMEM((ncell, sols), F32),
            pltpu.VMEM((ncell, sols), BF16),
            pltpu.VMEM((ncell, sols), BF16),
            pltpu.VMEM((parts * seg, sols), F32),
            pltpu.VMEM((ITERS, PARTS * seg, sols), F32),
            pltpu.VMEM((ITERS, PARTS * seg, sols), F32),
            dma((chunks,)),
            dma((nb, chunks)),
            dma((nb, chunks)),
            dma((nd, parts)),
            dma((nd, parts)),
            dma((ITERS, 2, PARTS)),
            dma((ITERS, 2, PARTS)),
        ],
        compiler_params=pltpu.CompilerParams(
            collective_id=0, has_side_effects=True, vmem_limit_bytes=60 * 1024 * 1024
        ),
        name="invert",
    )(sensitivity, observed, models, neighbour_map.T, edge_mask[:, None])


def solution(mesh):
    return jax.shard_map(
        functools.partial(invert, mesh.shape["dp"], mesh.shape["cells"]),
        mesh=mesh,
        in_specs=(P("dp", "cells"), P("dp", None), P("cells", None), P(), P("cells")),
        out_specs=P("cells", None),
        check_vma=False,
    )
```

time: 426 us -> 238 us (0.56); the launches traced: 419 us -> 238 us
  waiting for transfers between devices: 256 us -> 0 us
  Pallas kernels: 0 us -> 232 us
  matrix products: 77 us -> 0 us
  local copies, waits for them, and re-layouts: 41.2 us -> 6.13 us
  other arithmetic: 17.9 us -> 0 us
  between operations: 13.7 us -> 0.01 us
  starting transfers between devices: 12.6 us -> 0 us
    psum x4 -> x0, waiting for transfers between devices: 256 us -> none  [the longest x2 187 us: local(): lax.psum(jnp.dot(sensitivity, current, precision=lax.Precision.HIGHEST, p...]
    pallas_call x0 -> x1, Pallas kernels: none -> 232 us  [invert(): pl.pallas_call(functools.partial(body, (n_dp, n_cells), plane), out_shape...]
    dot_general x4 -> x0, matrix products: 77 us -> none  [the longest x2 49.5 us: local(): lax.dot_general(sensitivity, weighted, (((0,), (0,)), ((), ())), precisio...]
    gather x8 -> x0, local copies, waits for them, and re-layouts: 32.2 us -> none  [smooth_local(): other = jnp.take(planes, neighbour_map[k], axis=1)]
    ppermute x4 -> x0, starting transfers between devices: 12.5 us -> none  [the longest x2 9.95 us: with_halo(): lax.ppermute(tail, axis, [(i, (i + 1) % count) for i in range(ends)])]
    mul x2 -> x0, other arithmetic: 12.4 us -> none  [local(): current = current - 1.0 * gradient + 0.05 * smooth]
    add x2 -> x0, other arithmetic: 5.51 us -> none  [local(): current = current - 1.0 * gradient + 0.05 * smooth]
  transfers between devices with their start and end apart: 8 -> 0, of which waited for: 4 -> 0; matrix products, arithmetic and copies ran while one was open for 24% -> 0% of each run, Pallas kernels for 0% -> 0%
where the time goes in v1:
time: 238 us
  Pallas kernels  232 us (97%)
  local copies, waits for them, and re-layouts  6.13 us (3%)
    pallas_call x1, Pallas kernels, invert(): pl.pallas_call(functools.partial(body, (n_dp, n_cells), plane), out_shape...  232 us

profile of v1, /device:TPU:0, one launch (start us, length us, event | category | flops | bytes accessed | tf_op | source)
XLA Modules:
  0.0 238.1 jit_solution(4726341907749393975)
XLA Ops:
  0.0 1.6 copy.7
  1.6 1.8 broadcast_in_dim.4.mask_ref
  3.5 231.9 %invert.1 = f32[1536,256]{1,0:T(8,128)} custom-call(f32[2048,1536]{1,0:T(8,128)} %sens_hbm.1, f32[2048,256]{1,0:T(8,128)} %obs_ref.1, f32[1536,256]{1,0:T(8,128)} %models_ref.1, s32[768,4]{1,0:T(8,128)} %bitcast.1, s32[1536,1]{1,0:T(8,128)} %broadcast_in_dim.4.mask_ref), custom_call_target="tpu_custom_call" | custom-call | tf_op jit(solution)/shard_map/invert/pallas_call | solution.py:302
  235.4 2.7 %copy.10 = f32[1536,256]{1,0:T(8,128)} copy(f32[1536,256]{1,0:T(8,128)} %invert.1) | data formatting | bytes 3145728

commit v2 on v0

v2 whole, which is shorter than its diff:
```python
import functools

import jax
import jax.numpy as jnp
from jax import lax
from jax.experimental import pallas as pl
from jax.experimental.pallas import tpu as pltpu
from jax.sharding import PartitionSpec as P

ITERS = 2
CHUNK = 256
PARTS = 1
HALVES = 2
F32 = jnp.float32
BF16 = jnp.bfloat16


def split(x):
    hi = x.astype(BF16)
    return hi, (x - hi.astype(F32)).astype(BF16)


def digits_of(count, first):
    digits = []
    while count > 1:
        digits.append(first if not digits else min(4, count))
        count //= digits[-1]
    return digits


def radix(n_dp, n_cells):
    return digits_of(n_dp, 2), digits_of(n_cells, 2)


def dot(a, b, dims):
    return lax.dot_general(a, b, (dims, ((), ())), preferred_element_type=F32)


def aligned(start, size):
    return pl.ds(pl.multiple_of(start, 8), size)


class Scatter:
    def __init__(self, axis, digits, rows, sends, recvs):
        self.axis, self.rows, self.digits = axis, rows, digits
        self.sends, self.recvs = sends, recvs
        self.levels = len(digits)
        self.stages = 2 * self.levels
        me = lax.axis_index(axis)
        self.peer, self.away, self.off, self.size, self.sem = [], [], [0], [rows], []
        stride, sem = 1, 0
        for b, base in enumerate(digits):
            mine = (me // stride) % base
            piece = self.size[b] // base
            others = [(mine + j) % base for j in range(1, base)]
            self.peer.append([me + (v - mine) * stride for v in others])
            self.away.append([self.off[b] + v * piece for v in others])
            self.off.append(self.off[b] + mine * piece)
            self.size.append(piece)
            self.sem.append(sem)
            sem += base - 1
            stride *= base
        self.copies = sem

    def kept(self, chunk, b):
        return aligned(chunk * self.rows + self.off[b + 1], self.size[b + 1])

    def landed(self, chunk, b, j):
        at = self.rows - self.size[b] + j * self.size[b + 1]
        return aligned(chunk * self.rows + at, self.size[b + 1])

    def remote(self, source, target, slot, sem, peer):
        return pltpu.make_async_remote_copy(
            src_ref=source,
            dst_ref=target,
            send_sem=self.sends.at[sem, slot],
            recv_sem=self.recvs.at[sem, slot],
            device_id={self.axis: peer},
            device_id_type=pl.DeviceIdType.MESH,
        )

    def reduces(self, data, land, chunk, slot, b):
        for j in range(self.digits[b] - 1):
            source = data.at[aligned(chunk * self.rows + self.away[b][j], self.size[b + 1])]
            target = land.at[self.landed(chunk, b, j)]
            yield self.remote(source, target, slot, self.sem[b] + j, self.peer[b][j])

    def gathers(self, data, chunk, slot, b):
        here = data.at[self.kept(chunk, b)]
        for j in range(self.digits[b] - 1):
            yield self.remote(here, here, slot, self.copies + self.sem[b] + j, self.peer[b][j])

    def stage(self, s, chunk, slot, data, land, result, finish):
        levels = self.levels
        if 0 < s <= levels:
            b = s - 1
            for copy in self.reduces(data, land, chunk, slot, b):
                copy.wait()
            kept = self.kept(chunk, b)
            total = data[kept, :]
            for j in range(self.digits[b] - 1):
                total += land[self.landed(chunk, b, j), :]
            if s < levels:
                data[kept, :] = total
            else:
                finish(kept, total)
        elif s > levels:
            for copy in self.gathers(result, chunk, slot, 2 * levels - s):
                copy.wait()
        if s < levels:
            for copy in self.reduces(data, land, chunk, slot, s):
                copy.start()
        elif s < 2 * levels:
            for copy in self.gathers(result, chunk, slot, 2 * levels - 1 - s):
                copy.start()


def body(sizes, plane, sens_hbm, obs_hbm, models_hbm, near_ref, mask_ref, out_hbm,
         sens, obs, part, land, weighted, grad, gland, state, high, low, smooth,
         under, over, load_sem, obs_sem, edge_sem, c_send, c_recv, d_send, d_recv, h_send, h_recv):
    n_dp, n_cells = sizes
    ndata, ncell = sens.shape
    halves, _, width = grad.shape
    me = lax.axis_index("cells")
    chunks = c_send.shape[1] // halves
    rows = ndata // chunks
    parts = d_send.shape[1] // halves
    prow = ncell // parts
    per_plane = plane // prow
    dp_digits, cell_digits = radix(n_dp, n_cells)
    cells = Scatter("cells", cell_digits, rows, c_send, c_recv)
    dp = Scatter("dp", dp_digits, prow, d_send, d_recv)
    seg = dp.size[-1]
    own = dp.off[-1]
    units = halves * chunks
    delay = chunks + cells.stages
    period = delay + parts + dp.stages
    slots = (ITERS - 1) * period + delay + units - chunks + parts + dp.stages
    nn, tn = ((1,), (0,)), ((0,), (0,))

    def load(c):
        at = aligned(c * rows, rows)
        return pltpu.make_async_copy(sens_hbm.at[at], sens.at[at], load_sem.at[c])

    def columns(h):
        return pl.ds(h * width, width)

    def enter(h):
        return pltpu.make_async_copy(models_hbm.at[:, columns(h)], state.at[0, h], edge_sem.at[h])

    def leave(h):
        return pltpu.make_async_copy(state.at[ITERS, h], out_hbm.at[:, columns(h)], edge_sem.at[h])

    def watch(h):
        return pltpu.make_async_copy(obs_hbm.at[:, columns(h)], obs.at[h], obs_sem.at[h])

    for h in range(halves):
        enter(h).start()
    for c in range(chunks):
        load(c).start()
    for h in range(halves):
        watch(h).start()

    barrier = pltpu.get_barrier_semaphore()

    def greet(where):
        pl.semaphore_signal(barrier, inc=1, device_id=where, device_id_type=pl.DeviceIdType.MESH)

    for peers in cells.peer:
        for peer in peers:
            greet({"cells": peer})
    for peers in dp.peer:
        for peer in peers:
            greet({"dp": peer})

    has_under, has_over = me > 0, me < n_cells - 1

    @pl.when(has_under)
    def _():
        greet({"cells": me - 1})

    @pl.when(has_over)
    def _():
        greet({"cells": me + 1})

    @pl.when(me == 0)
    def _():
        under[...] = jnp.zeros_like(under)

    @pl.when(me == n_cells - 1)
    def _():
        over[...] = jnp.zeros_like(over)

    for h in range(halves):
        enter(h).wait()

    pl.semaphore_wait(
        barrier,
        cells.copies + dp.copies + (me + n_cells - 1) // n_cells + (2 * n_cells - 2 - me) // n_cells,
    )

    def halo(step, h, i, upward):
        source = (ncell - plane if upward else 0) + i * prow + own
        return pltpu.make_async_remote_copy(
            src_ref=state.at[step, h, aligned(source, seg)],
            dst_ref=(under if upward else over).at[step, h, pl.ds(i * seg, seg)],
            send_sem=h_send.at[step, h, int(upward) * per_plane + i],
            recv_sem=h_recv.at[step, h, int(upward) * per_plane + i],
            device_id={"cells": me + 1 if upward else me - 1},
            device_id_type=pl.DeviceIdType.MESH,
        )

    def halos(act_over, act_under):
        @pl.when(has_over)
        def _():
            for i in range(per_plane):
                act_over(i)

        @pl.when(has_under)
        def _():
            for i in range(per_plane):
                act_under(i)

    def predict(step, h, c):
        @pl.when(c == 0)
        def _():
            halos(
                lambda i: halo(step, h, i, True).start(),
                lambda i: halo(step, h, i, False).start(),
            )
            hi, lo = split(state[step, h])
            high[h] = hi
            low[h] = lo

        @pl.when(jnp.logical_and(step == 0, h == 0))
        def _():
            load(c).wait()

        at = aligned(c * rows, rows)
        s_hi, s_lo = split(sens[at, :])
        part[h, at, :] = dot(s_hi, high[h], nn) + dot(s_hi, low[h], nn) + dot(s_lo, high[h], nn)

    def back(step, h, c):
        @pl.when(c == 0)
        def _():
            grad[h] = jnp.zeros_like(grad[h])

        at = aligned(c * rows, rows)
        s_hi, s_lo = split(sens[at, :])
        w_hi, w_lo = split(weighted[h, at, :])
        grad[h] += dot(s_hi, w_hi, tn) + dot(s_hi, w_lo, tn) + dot(s_lo, w_hi, tn)

    def smooth_part(step, h, q):
        @pl.when(q == 0)
        def _():
            halos(
                lambda i: halo(step, h, i, True).wait_send(),
                lambda i: halo(step, h, i, False).wait_send(),
            )
            halos(
                lambda i: halo(step, h, i, False).wait_recv(),
                lambda i: halo(step, h, i, True).wait_recv(),
            )

        base = q * prow + own
        inner = lax.rem(base, plane)
        first = base - inner
        cell = state[step, h, aligned(base, seg), :]
        total = jnp.zeros_like(cell)

        def add(other):
            diff = other - cell
            return diff / jnp.sqrt(1.0 + diff * diff)

        at = aligned(lax.rem(q, per_plane) * seg, seg)
        below = state[step, h, aligned(jnp.maximum(base - plane, 0), seg), :]
        above = state[step, h, aligned(jnp.minimum(base + plane, ncell - seg), seg), :]
        total += add(jnp.where(first == 0, under[step, h, at, :], below))
        total += add(jnp.where(first == ncell - plane, over[step, h, at, :], above))
        whole = pl.ds(pl.multiple_of(first, 16), plane)
        for k in range(4):
            column = near_ref[aligned(inner, seg), k:k + 1]
            pick = column == lax.broadcasted_iota(jnp.int32, (seg, plane), 1)
            pick = jnp.where(pick, 1.0, 0.0).astype(BF16)
            total += add(dot(pick, high[h, whole, :], nn) + dot(pick, low[h, whole, :], nn))
        scale = 1.0 - 0.75 * mask_ref[aligned(base, seg), :].astype(F32)
        smooth[h, aligned(q * seg, seg), :] = total * scale

    def at_slot(x, count, act):
        step, unit = lax.div(x, period), lax.rem(x, period)
        h, index = lax.div(unit, chunks), lax.rem(unit, chunks)

        @pl.when((x >= 0) & (step < ITERS) & (unit < units) & (index < count))
        def _():
            act(step, h, index)

    def cell_stage(s, step, h, c):
        def reweight(kept, total):
            misfit = total - obs[h, kept, :]
            weighted[h, kept, :] = misfit / jnp.maximum(jnp.abs(misfit), 1.0)

        cells.stage(s, c, h * chunks + c, part.at[h], land.at[h], weighted.at[h], reweight)

    def dp_stage(s, step, h, q):
        def update(kept, total):
            moved = state[step, h, kept, :] - 1.0 * total
            state[step + 1, h, kept, :] = moved + 0.05 * smooth[h, aligned(q * seg, seg), :]

        dp.stage(s, q, h * parts + q, grad.at[h], gland.at[h], state.at[step + 1, h], update)

    def slot(t, carry):
        @pl.when(t == 0)
        def _():
            for h in range(halves):
                watch(h).wait()

        for s in reversed(range(cells.stages + 1)):
            at_slot(t - s, chunks, functools.partial(cell_stage, s))
        for s in reversed(range(dp.stages + 1)):
            at_slot(t - delay - s, parts, functools.partial(dp_stage, s))
        at_slot(t + 1, chunks, predict)
        at_slot(t - 2, parts, smooth_part)
        at_slot(t - cells.stages, chunks, back)
        return carry

    lax.fori_loop(-1, slots, slot, 0)
    for h in range(halves):
        leave(h).start()
    for h in range(halves):
        leave(h).wait()


def invert(n_dp, n_cells, sensitivity, observed, models, neighbour_map, edge_mask):
    ndata, ncell = sensitivity.shape
    width = models.shape[1] // HALVES
    plane = neighbour_map.shape[1]
    rows = max(CHUNK, 8 * n_cells)
    chunks = ndata // rows
    parts = ncell // plane * PARTS
    seg = ncell // parts // n_dp
    vmem = pl.BlockSpec(memory_space=pltpu.VMEM)
    hbm = pl.BlockSpec(memory_space=pl.ANY)
    dma = pltpu.SemaphoreType.DMA
    nd, nb = (2 * sum(d - 1 for d in digits) for digits in radix(n_dp, n_cells))
    return pl.pallas_call(
        functools.partial(body, (n_dp, n_cells), plane),
        out_shape=jax.ShapeDtypeStruct(models.shape, F32),
        in_specs=[hbm] * 3 + [vmem] * 2,
        out_specs=hbm,
        scratch_shapes=[
            pltpu.VMEM((ndata, ncell), F32),
            pltpu.VMEM((HALVES, ndata, width), F32),
            pltpu.VMEM((HALVES, ndata, width), F32),
            pltpu.VMEM((HALVES, ndata, width), F32),
            pltpu.VMEM((HALVES, ndata, width), F32),
            pltpu.VMEM((HALVES, ncell, width), F32),
            pltpu.VMEM((HALVES, ncell, width), F32),
            pltpu.VMEM((ITERS + 1, HALVES, ncell, width), F32),
            pltpu.VMEM((HALVES, ncell, width), BF16),
            pltpu.VMEM((HALVES, ncell, width), BF16),
            pltpu.VMEM((HALVES, parts * seg, width), F32),
            pltpu.VMEM((ITERS, HALVES, PARTS * seg, width), F32),
            pltpu.VMEM((ITERS, HALVES, PARTS * seg, width), F32),
            dma((chunks,)),
            dma((HALVES,)),
            dma((HALVES,)),
            dma((nb, HALVES * chunks)),
            dma((nb, HALVES * chunks)),
            dma((nd, HALVES * parts)),
            dma((nd, HALVES * parts)),
            dma((ITERS, HALVES, 2 * PARTS)),
            dma((ITERS, HALVES, 2 * PARTS)),
        ],
        compiler_params=pltpu.CompilerParams(
            collective_id=0, has_side_effects=True, vmem_limit_bytes=60 * 1024 * 1024
        ),
        name="invert",
    )(sensitivity, observed, models, neighbour_map.T, edge_mask[:, None])


def solution(mesh):
    return jax.shard_map(
        functools.partial(invert, mesh.shape["dp"], mesh.shape["cells"]),
        mesh=mesh,
        in_specs=(P("dp", "cells"), P("dp", None), P("cells", None), P(), P("cells")),
        out_specs=P("cells", None),
        check_vma=False,
    )
```

time: 426 us -> 205 us (0.48); the launches traced: 419 us -> 204 us
  waiting for transfers between devices: 256 us -> 0 us
  Pallas kernels: 0 us -> 198 us
  matrix products: 77 us -> 0 us
  local copies, waits for them, and re-layouts: 41.2 us -> 6.13 us
  other arithmetic: 17.9 us -> 0 us
  between operations: 13.7 us -> 0.01 us
  starting transfers between devices: 12.6 us -> 0 us
    psum x4 -> x0, waiting for transfers between devices: 256 us -> none  [the longest x2 187 us: local(): lax.psum(jnp.dot(sensitivity, current, precision=lax.Precision.HIGHEST, p...]
    pallas_call x0 -> x1, Pallas kernels: none -> 198 us  [invert(): pl.pallas_call(functools.partial(body, (n_dp, n_cells), plane), out_shape...]
    dot_general x4 -> x0, matrix products: 77 us -> none  [the longest x2 49.5 us: local(): lax.dot_general(sensitivity, weighted, (((0,), (0,)), ((), ())), precisio...]
    gather x8 -> x0, local copies, waits for them, and re-layouts: 32.2 us -> none  [smooth_local(): other = jnp.take(planes, neighbour_map[k], axis=1)]
    ppermute x4 -> x0, starting transfers between devices: 12.5 us -> none  [the longest x2 9.95 us: with_halo(): lax.ppermute(tail, axis, [(i, (i + 1) % count) for i in range(ends)])]
    mul x2 -> x0, other arithmetic: 12.4 us -> none  [local(): current = current - 1.0 * gradient + 0.05 * smooth]
    add x2 -> x0, other arithmetic: 5.51 us -> none  [local(): current = current - 1.0 * gradient + 0.05 * smooth]
  transfers between devices with their start and end apart: 8 -> 0, of which waited for: 4 -> 0; matrix products, arithmetic and copies ran while one was open for 24% -> 0% of each run, Pallas kernels for 0% -> 0%
where the time goes in v2:
time: 205 us; the launch traced here: 204 us
  Pallas kernels  198 us (97%)
  local copies, waits for them, and re-layouts  6.13 us (3%)
    pallas_call x1, Pallas kernels, invert(): pl.pallas_call(functools.partial(body, (n_dp, n_cells), plane), out_shape...  198 us
    unnamed x2, local copies, waits for them, and re-layouts  4.28 us

profile of v2, /device:TPU:0, one launch (start us, length us, event | category | flops | bytes accessed | tf_op | source)
XLA Modules:
  0.0 204.5 jit_solution(13821387269211503797)
XLA Ops:
  0.0 1.6 copy.7
  1.6 1.8 broadcast_in_dim.4.mask_ref
  3.5 198.4 %invert.1 = f32[1536,256]{1,0:T(8,128)} custom-call(f32[2048,1536]{1,0:T(8,128)} %sens_hbm.1, f32[2048,256]{1,0:T(8,128)} %obs_hbm.1, f32[1536,256]{1,0:T(8,128)} %models_hbm.1, s32[768,4]{1,0:T(8,128)} %bitcast.1, s32[1536,1]{1,0:T(8,128)} %broadcast_in_dim.4.mask_ref), custom_call_target="tpu_custom_call" | custom-call | tf_op jit(solution)/shard_map/invert/pallas_call | solution.py:345
  201.8 2.7 %copy.10 = f32[1536,256]{1,0:T(8,128)} copy(f32[1536,256]{1,0:T(8,128)} %invert.1) | data formatting | bytes 3145728

commit v3 on v2

--- a/solution.py
+++ b/solution.py
@@ -11,6 +11,9 @@
 CHUNK = 256
 PARTS = 1
 HALVES = 2
+LAG = 3
+DP_LAG = 3
+RADIX = 2
 F32 = jnp.float32
 BF16 = jnp.bfloat16
 
@@ -23,7 +26,7 @@
 def digits_of(count, first):
     digits = []
     while count > 1:
-        digits.append(first if not digits else min(4, count))
+        digits.append(first if not digits else min(RADIX, count))
         count //= digits[-1]
     return digits
 
@@ -133,9 +136,9 @@
     seg = dp.size[-1]
     own = dp.off[-1]
     units = halves * chunks
-    delay = chunks + cells.stages
-    period = delay + parts + dp.stages
-    slots = (ITERS - 1) * period + delay + units - chunks + parts + dp.stages
+    delay = chunks + LAG * cells.stages
+    period = delay + parts + DP_LAG * dp.stages
+    slots = (ITERS - 1) * period + delay + units - chunks + parts + DP_LAG * dp.stages
     nn, tn = ((1,), (0,)), ((0,), (0,))
 
     def load(c):
@@ -315,12 +318,12 @@
                 watch(h).wait()
 
         for s in reversed(range(cells.stages + 1)):
-            at_slot(t - s, chunks, functools.partial(cell_stage, s))
+            at_slot(t - LAG * s, chunks, functools.partial(cell_stage, s))
         for s in reversed(range(dp.stages + 1)):
-            at_slot(t - delay - s, parts, functools.partial(dp_stage, s))
+            at_slot(t - delay - DP_LAG * s, parts, functools.partial(dp_stage, s))
         at_slot(t + 1, chunks, predict)
         at_slot(t - 2, parts, smooth_part)
-        at_slot(t - cells.stages, chunks, back)
+        at_slot(t - LAG * cells.stages, chunks, back)
         return carry
 
     lax.fori_loop(-1, slots, slot, 0)

time: 205 us -> 160 us (0.78)
  Pallas kernels: 198 us -> 153 us
    pallas_call x1, Pallas kernels: 198 us -> 153 us  [invert(): pl.pallas_call(functools.partial(body, (n_dp, n_cells), plane), out_shape...]
where the time goes in v3:
time: 160 us; the launch traced here: 159 us
  Pallas kernels  153 us (96%)
  local copies, waits for them, and re-layouts  6.13 us (4%)
    pallas_call x1, Pallas kernels, invert(): pl.pallas_call(functools.partial(body, (n_dp, n_cells), plane), out_shape...  153 us
    unnamed x2, local copies, waits for them, and re-layouts  4.28 us

profile of v3, /device:TPU:0, one launch (start us, length us, event | category | flops | bytes accessed | tf_op | source)
XLA Modules:
  0.0 159.5 jit_solution(4221420902197793169)
XLA Ops:
  0.0 1.6 %copy.7 = s32[4,768]{0,1:T(8,128)} copy(s32[4,768]{1,0:T(4,128)} %param.8) | data formatting | bytes 24576 | tf_op args[3]
  1.6 1.8 %broadcast_in_dim.4.mask_ref = s32[1536,1]{1,0:T(8,128)} reshape(s32[1536]{0:T(1024)} %param.9) | data formatting | bytes 12288 | tf_op jit(solution)/shard_map/broadcast_in_dim | solution.py:381
  3.5 153.3 %invert.1 = f32[1536,256]{1,0:T(8,128)} custom-call(f32[2048,1536]{1,0:T(8,128)} %sens_hbm.1, f32[2048,256]{1,0:T(8,128)} %obs_hbm.1, f32[1536,256]{1,0:T(8,128)} %models_hbm.1, s32[768,4]{1,0:T(8,128)} %bitcast.1, s32[1536,1]{1,0:T(8,128)} %broadcast_in_dim.4.mask_ref), custom_call_target="tpu_custom_call" | custom-call | tf_op jit(solution)/shard_map/invert/pallas_call | solution.py:348
  156.8 2.7 %copy.10 = f32[1536,256]{1,0:T(8,128)} copy(f32[1536,256]{1,0:T(8,128)} %invert.1) | data formatting | bytes 3145728
